TPU v7x, 32 devices: a whole 2x2x4 slice. The times are simulated.
32 devices in a mesh: row: 4 (over y, x), col: 8 (over z, core).
Axes of the slice: x: 2, y: 2, z: 4, core: 2. Of those that a mesh axis runs over, the one named last changes fastest.
Arguments:
- b_steps: float32 [2, 1024, 2048], P(None, 'row', 'col'), may hold values from -6 to 6
- b_trail: float32 [4096, 2048], P('row', 'col'), may hold values from -6 to 6
- l_cross: float32 [1024, 1024], P('row', 'col'), may hold values from -0.1875 to 0.1875
- l_trail: float32 [2, 4096, 1024], P(None, 'row', 'col'), may hold values from -0.125 to 0.125
- diag_inv: float32 [2, 2, 512, 512], P(None, None, None, 'col'), may hold values from -1.5 to 1.5, as said below
- diag_low: float32 [2, 512, 512], P(None, None, 'col'), may hold values from -0.25 to 0.25
Outputs:
- x_steps: float32 [2, 1024, 2048], P(None, 'row', 'col')
- trail_out: float32 [4096, 2048], P('row', 'col')
Inputs may be any that keep to these rules, and one draw needn't show every extreme that they name: Each diag_inv[s, h] is lower triangular with diagonal entries of 0.5 to 1.5 and strictly lower entries of magnitude at most 3 / sqrt(512).
All inputs are finite; a program needn't handle non-finite values.
Results may differ from a plain program's by a relative error of at most 0.00013.
Values sent between devices are 32-bit elements; how exact they have to be, the bound alone decides.
No kernel may reach another device: no remote copies, remote signals or barrier semaphores. Data moves between devices by JAX's collectives and lax.ppermute only.
A program may use at most 64 MiB of HBM per device.

v0:
```python
import jax
import jax.numpy as jnp
from jax import lax
from jax.sharding import PartitionSpec as P

exact_prec = lax.Precision.HIGHEST


def mult(left_mat, right_mat):
    return jnp.dot(left_mat, right_mat, precision=exact_prec, preferred_element_type=jnp.float32)


def inverse_columns(diag_inv, diag_low, section, offset, own_rows):
    inv_first = diag_inv[section, 0]
    inv_second = diag_inv[section, 1]
    low_block = diag_low[section]
    first_all, second_all, low_all = (
        lax.all_gather(inv_first, "col", axis=1, tiled=True),
        lax.all_gather(inv_second, "col", axis=1, tiled=True),
        lax.all_gather(low_block, "col", axis=1, tiled=True),
    )
    half_rows = first_all.shape[0]
    first_at = jnp.minimum(offset, half_rows - own_rows)
    chosen = lax.dynamic_slice_in_dim(first_all, first_at, own_rows, 1)
    upper = jnp.concatenate([chosen, -mult(second_all, mult(low_all, chosen))], 0)
    second_at = jnp.clip(offset - half_rows, 0, half_rows - own_rows)
    picked = lax.dynamic_slice_in_dim(second_all, second_at, own_rows, 1)
    bottom = jnp.concatenate([jnp.zeros((half_rows, own_rows), jnp.float32), picked], 0)
    return jnp.where(offset < half_rows, upper, bottom)


def solve_step(diag_inv, diag_low, section, offset, own_rows, rows_block):
    inverse_cols = inverse_columns(diag_inv, diag_low, section, offset, own_rows)
    return lax.psum(mult(inverse_cols, rows_block), "row")


def shards(b_steps, b_trail, l_cross, l_trail, diag_inv, diag_low):
    own_rows = b_steps.shape[1]
    offset = lax.axis_index("row") * own_rows
    solved_first = solve_step(diag_inv, diag_low, 0, offset, own_rows, b_steps[0])
    segment = solved_first
    next_rows = b_steps[1] - mult(lax.all_gather(l_cross, "col", axis=1, tiled=True), segment)
    trail = b_trail - mult(lax.all_gather(l_trail[0], "col", axis=1, tiled=True), segment)
    solved_second = solve_step(diag_inv, diag_low, 1, offset, own_rows, next_rows)
    segment = solved_second
    trail = trail - mult(lax.all_gather(l_trail[1], "col", axis=1, tiled=True), segment)
    mine_first = lax.dynamic_slice_in_dim(solved_first, offset, own_rows, 0)
    mine_second = lax.dynamic_slice_in_dim(solved_second, offset, own_rows, 0)
    return (jnp.stack([mine_first, mine_second]), trail)


def solution(mesh):
    placed = (
        P(None, "row", "col"),
        P("row", "col"),
        P("row", "col"),
        P(None, "row", "col"),
        P(None, None, None, "col"),
        P(None, None, "col"),
    )
    return jax.shard_map(
        shards,
        mesh=mesh,
        in_specs=placed,
        out_specs=(P(None, "row", "col"), P("row", "col")),
        check_vma=False,
    )
```

profile of v0, /device:TPU:0, one launch (start us, length us, event | category | flops | bytes accessed | tf_op | source)
XLA Modules:
  0.0 404.8 jit_solution(14901719577600979641)
XLA Ops:
  7.2 1.9 fusion.42
  10.0 1.7 fusion.43
  14.3 20.3 %all-gather.20.cloned.1.call-done = f32[1,1,512,512]{2,3,1,0:T(8,128)} async-done(((f32[1,1,512,64]{2,3,1,0:T(8,128)}), f32[1,1,512,512]{2,3,1,0:T(8,128)}) %all-gather.20.cloned.1.call-update) | async-done | bytes 1048592 | tf_op jit(solution)/shard_map/all_gather | solution.py:18
  35.7 22.9 %all-gather.24.cloned.1.call-done = f32[1,1,512,512]{2,3,1,0:T(8,128)} async-done(((f32[1,1,512,64]{2,3,1,0:T(8,128)}), f32[1,1,512,512]{2,3,1,0:T(8,128)}) %all-gather.24.cloned.1.call-update) | async-done | bytes 1048592 | tf_op jit(solution)/shard_map/all_gather | solution.py:19
  59.7 22.4 %all-gather.22.cloned.1.call-done = f32[1,512,512]{1,2,0:T(8,128)} async-done(((f32[1,512,64]{1,2,0:T(8,128)}), f32[1,512,512]{1,2,0:T(8,128)}) %all-gather.22.cloned.1.call-update) | async-done | bytes 1048592 | tf_op jit(solution)/shard_map/all_gather | solution.py:20
  82.1 2.3 fusion.29
  84.4 2.3 fusion.17
  86.7 2.8 fusion.19
  89.5 15.9 %all-gather.26.cloned.1.call-done = f32[1,1,512,512]{2,3,1,0:T(8,128)} async-done(((f32[1,1,512,64]{2,3,1,0:T(8,128)}), f32[1,1,512,512]{2,3,1,0:T(8,128)}) %all-gather.26.cloned.1.call-update) | async-done | bytes 1048592 | tf_op jit(solution)/shard_map/all_gather | solution.py:18
  106.6 22.8 %all-gather.30.cloned.1.call-done = f32[1,1,512,512]{2,3,1,0:T(8,128)} async-done(((f32[1,1,512,64]{2,3,1,0:T(8,128)}), f32[1,1,512,512]{2,3,1,0:T(8,128)}) %all-gather.30.cloned.1.call-update) | async-done | bytes 1048592 | tf_op jit(solution)/shard_map/all_gather | solution.py:19
  130.5 22.2 %all-gather.28.cloned.1.call-done = f32[1,512,512]{1,2,0:T(8,128)} async-done(((f32[1,512,64]{1,2,0:T(8,128)}), f32[1,512,512]{1,2,0:T(8,128)}) %all-gather.28.cloned.1.call-update) | async-done | bytes 1048592 | tf_op jit(solution)/shard_map/all_gather | solution.py:20
  152.7 2.3 fusion.26
  155.0 2.3 fusion.16
  157.2 20.6 %all-gather.18.cloned.1.call-done = f32[256,1024]{1,0:T(8,128)} async-done(((f32[256,128]{1,0:T(8,128)}), f32[256,1024]{1,0:T(8,128)}) %all-gather.18.cloned.1.call-update) | async-done | bytes 1048592 | tf_op jit(solution)/shard_map/all_gather | solution.py:42
  177.8 54.9 %all-reduce.5.cloned.1.call-done = f32[1024,256]{1,0:T(8,128)} async-done(((f32[1024,256]{1,0:T(8,128)}), f32[1024,256]{1,0:T(8,128)}) %all-reduce.5.cloned.1.call-update) | async-done | bytes 1048592 | tf_op jit(solution)/shard_map/psum | solution.py:34
  232.7 2.6 fusion.18
  235.3 2.8 fusion.22
  238.1 2.3 fusion.41
  241.6 49.1 %all-reduce.7.cloned.1.call-done = f32[1024,256]{1,0:T(8,128)} async-done(((f32[1024,256]{1,0:T(8,128)}), f32[1024,256]{1,0:T(8,128)}) %all-reduce.7.cloned.1.call-update) | async-done | bytes 1048592 | tf_op jit(solution)/shard_map/psum | solution.py:34
  292.5 47.5 %all-gather.34.cloned.1.call-done = f32[1,1024,1024]{2,1,0:T(8,128)} async-done(((f32[1,1024,128]{2,1,0:T(8,128)}), f32[1,1024,1024]{2,1,0:T(8,128)}) %all-gather.34.cloned.1.call-update) | async-done | bytes 4194320 | tf_op jit(solution)/shard_map/all_gather | solution.py:46
  340.0 10.3 %fusion.13 = f32[1024,256]{0,1:T(8,128)} fusion(f32[1024,256]{1,0:T(8,128)} %all-reduce.7.cloned.1.call-done, f32[1,1024,1024]{2,1,0:T(8,128)} %all-gather.34.cloned.1.call-done), kind=kOutput, calls=%fused_computation.7 | convolution fusion | flops 3221225472 | bytes 6291456 | tf_op jit(solution)/shard_map/dot_general | solution.py:10
  350.3 37.3 %all-gather.32.cloned.1.call-done = f32[1,1024,1024]{2,1,0:T(8,128)} async-done(((f32[1,1024,128]{2,1,0:T(8,128)}), f32[1,1024,1024]{2,1,0:T(8,128)}) %all-gather.32.cloned.1.call-update) | async-done | bytes 4194320 | tf_op jit(solution)/shard_map/all_gather | solution.py:43
  387.6 9.3 %fusion.10 = f32[1024,256]{0,1:T(8,128)S(1)} fusion(f32[1024,256]{0,1:T(8,128)} %fusion.13, f32[1024,256]{0,1:T(8,128)S(1)} %copy.8, f32[1024,256]{1,0:T(8,128)S(1)} %copy-done, f32[1,1024,1024]{2,1,0:T(8,128)} %all-gather.32.cloned.1.call-done), kind=kOutput, calls=%fused_computation.6 | convolution fusion | flops 3221749760 | bytes 8388608 | tf_op jit(solution)/shard_map/dot_general | solution.py:10
  396.9 1.3 copy.9
  (36 shorter events, 10.8 us)
Async XLA Ops:
  7.2 79.5 %copy-start.2 = (f32[2,256,256]{2,1,0:T(8,128)S(1)}, f32[2,256,256]{2,1,0:T(8,128)}, u32[]{:S(2)}) copy-start(f32[2,256,256]{2,1,0:T(8,128)} %param.6) | copy-start | bytes 1572868
  7.2 27.4 %all-gather.20.cloned.1.call-start = ((), (), s32[]{:S(2)}) async-start(), calls=%async_computation.3 | async-start | bytes 1179648 | tf_op jit(solution)/shard_map/all_gather | solution.py:18
  9.2 49.5 %all-gather.24.cloned.1.call-start = ((), (), s32[]{:S(2)}) async-start(), calls=%async_computation.5 | async-start | bytes 1179648 | tf_op jit(solution)/shard_map/all_gather | solution.py:19
  9.9 72.2 %all-gather.22.cloned.1.call-start = ((), (), s32[]{:S(2)}) async-start(), calls=%async_computation.4 | async-start | bytes 1179648 | tf_op jit(solution)/shard_map/all_gather | solution.py:20
  11.7 93.7 %all-gather.26.cloned.1.call-start = ((), (), s32[]{:S(2)}) async-start(), calls=%async_computation.6 | async-start | bytes 1179648 | tf_op jit(solution)/shard_map/all_gather | solution.py:18
  12.3 117.0 %all-gather.30.cloned.1.call-start = ((), (), s32[]{:S(2)}) async-start(), calls=%async_computation.8 | async-start | bytes 1179648 | tf_op jit(solution)/shard_map/all_gather | solution.py:19
  12.9 139.8 %all-gather.28.cloned.1.call-start = ((), (), s32[]{:S(2)}) async-start(), calls=%async_computation.7 | async-start | bytes 1179648 | tf_op jit(solution)/shard_map/all_gather | solution.py:20
  13.5 164.3 %all-gather.18.cloned.1.call-start = ((), (), s32[]{:S(2)}) async-start(), calls=%async_computation.1 | async-start | bytes 1179648 | tf_op jit(solution)/shard_map/all_gather | solution.py:42
  14.2 218.5 %all-reduce.5.cloned.1.call-start = ((), (), s32[]{:S(2)}) async-start(), calls=%async_computation | async-start | bytes 2097152 | tf_op jit(solution)/shard_map/psum | solution.py:34
  89.5 201.2 %all-reduce.7.cloned.1.call-start = ((), (), s32[]{:S(2)}) async-start(), calls=%async_computation.2 | async-start | bytes 2097152 | tf_op jit(solution)/shard_map/psum | solution.py:34
  235.3 6.3 %copy-start = (f32[1024,256]{1,0:T(8,128)S(1)}, f32[1024,256]{1,0:T(8,128)}, u32[]{:S(2)}) copy-start(f32[1024,256]{1,0:T(8,128)} %all-reduce.5.cloned.1.call-done) | copy-start | bytes 3145732
  238.1 3.2 copy-start.1
  238.1 101.9 %all-gather.34.cloned.1.call-start = ((), (), s32[]{:S(2)}) async-start(), calls=%async_computation.10 | async-start | bytes 4718592 | tf_op jit(solution)/shard_map/all_gather | solution.py:46
  240.5 147.1 %all-gather.32.cloned.1.call-start = ((), (), s32[]{:S(2)}) async-start(), calls=%async_computation.9 | async-start | bytes 4718592 | tf_op jit(solution)/shard_map/all_gather | solution.py:43
Sparse Core Ops, SparseCore 0:
  9.6 24.9 all-gather.19
  36.7 21.8 all-gather.23
  60.2 21.8 all-gather.21
  83.6 21.8 all-gather.25
  107.5 21.8 all-gather.29
  130.8 21.8 all-gather.27
  154.3 23.4 all-gather.17
  181.4 51.1 all-reduce.4
  238.2 52.4 all-reduce.6
  292.2 47.8 all-gather.33
  341.6 45.9 all-gather.31
where the time goes:
time: 405 us
  waiting for transfers between devices  339 us (84%)
  matrix products  36.8 us (9%)
  between operations  14 us (3%)
  local copies, waits for them, and re-layouts  13 us (3%)
    psum x2, waiting for transfers between devices, solve_step(): return lax.psum(mult(inverse_cols, rows_block), 'row')  104 us
    all_gather x1, waiting for transfers between devices, shards(): lax.all_gather(l_trail[1], 'col', axis=1, tiled=True)  47.5 us
    all_gather x2, waiting for transfers between devices, inverse_columns(): lax.all_gather(inv_second, 'col', axis=1, tiled=True)  45.7 us
    all_gather x2, waiting for transfers between devices, inverse_columns(): lax.all_gather(low_block, 'col', axis=1, tiled=True)  44.6 us
    all_gather x1, waiting for transfers between devices, shards(): lax.all_gather(l_trail[0], 'col', axis=1, tiled=True)  37.3 us
    dot_general x9, matrix products, mult(): jnp.dot(left_mat, right_mat, precision=exact_prec, preferred_element_type...  36.8 us
    all_gather x2, waiting for transfers between devices, inverse_columns(): lax.all_gather(inv_first, 'col', axis=1, tiled=True)  36.2 us
    all_gather x1, waiting for transfers between devices, shards(): lax.all_gather(l_cross, 'col', axis=1, tiled=True)  20.6 us
  transfers between devices with their start and end apart: 11, of which 11 were waited for; matrix products, arithmetic and copies ran while one was open for 8% of the time, Pallas kernels for 0%

commit v1 on v0

--- a/solution.py
+++ b/solution.py
@@ -15,7 +15,9 @@
     inv_second = diag_inv[section, 1]
     low_block = diag_low[section]
     first_all, second_all, low_all = (
-        lax.all_gather(inv_first, "col", axis=1, tiled=True),
+        jnp.concatenate(
+            lax.all_to_all(jnp.stack([inv_first] * lax.axis_size("col")), "col", 0, 0), axis=1
+        ),
         lax.all_gather(inv_second, "col", axis=1, tiled=True),
         lax.all_gather(low_block, "col", axis=1, tiled=True),
     )

time: 405 us -> 375 us (0.926)
  waiting for transfers between devices: 339 us -> 299 us
  starting transfers between devices: 0.62 us -> 10.6 us
    all_to_all x0 -> x2, waiting for transfers between devices: none -> 49 us  [inverse_columns(): lax.all_to_all(jnp.stack([inv_first] * lax.axis_size('col')), 'col', 0, 0)]
    all_gather x2, waiting for transfers between devices: 45.7 us -> 7.51 us  [inverse_columns(): lax.all_gather(inv_second, 'col', axis=1, tiled=True)]
    all_gather x2 -> x0, waiting for transfers between devices: 36.2 us -> none  [inverse_columns(): lax.all_gather(inv_first, 'col', axis=1, tiled=True)]
    all_gather x2, waiting for transfers between devices: 44.6 us -> 31.4 us  [inverse_columns(): lax.all_gather(low_block, 'col', axis=1, tiled=True)]
    all_to_all x0 -> x2, starting transfers between devices: none -> 10 us  [inverse_columns(): lax.all_to_all(jnp.stack([inv_first] * lax.axis_size('col')), 'col', 0, 0)]
  transfers between devices with their start and end apart: 11 -> 11, of which waited for: 11 -> 10; matrix products, arithmetic and copies ran while one was open for 8% -> 9% of each run, Pallas kernels for 0% -> 0%
where the time goes in v1:
time: 375 us
  waiting for transfers between devices  299 us (80%)
  matrix products  36.8 us (10%)
  between operations  14 us (4%)
  local copies, waits for them, and re-layouts  13.1 us (3%)
  starting transfers between devices  10.6 us (3%)
    psum x2, waiting for transfers between devices, solve_step(): return lax.psum(mult(inverse_cols, rows_block), 'row')  104 us
    all_to_all x2, waiting for transfers between devices, inverse_columns(): lax.all_to_all(jnp.stack([inv_first] * lax.axis_size('col')), 'col', 0, 0)  49 us
    all_gather x1, waiting for transfers between devices, shards(): lax.all_gather(l_trail[1], 'col', axis=1, tiled=True)  47.6 us
    all_gather x1, waiting for transfers between devices, shards(): lax.all_gather(l_trail[0], 'col', axis=1, tiled=True)  37.3 us
    dot_general x9, matrix products, mult(): jnp.dot(left_mat, right_mat, precision=exact_prec, preferred_element_type...  36.8 us
    all_gather x2, waiting for transfers between devices, inverse_columns(): lax.all_gather(low_block, 'col', axis=1, tiled=True)  31.4 us
    all_gather x1, waiting for transfers between devices, shards(): lax.all_gather(l_cross, 'col', axis=1, tiled=True)  20.4 us
    all_to_all x2, starting transfers between devices, inverse_columns(): lax.all_to_all(jnp.stack([inv_first] * lax.axis_size('col')), 'col', 0, 0)  10 us
  transfers between devices with their start and end apart: 11, of which 10 were waited for; matrix products, arithmetic and copies ran while one was open for 9% of the time, Pallas kernels for 0%

profile of v1, /device:TPU:0, one launch (start us, length us, event | category | flops | bytes accessed | tf_op | source)
XLA Modules:
  0.0 374.8 jit_solution(11031896267655203985)
XLA Ops:
  7.2 1.8 fusion.42
  9.1 1.7 fusion.43
  13.3 6.4 %all-to-all-start = ((f32[8,512,64]{1,2,0:T(8,128)}), f32[8,512,64]{1,2,0:T(8,128)S(1)}, u32[]{:S(2)}, u32[]{:S(2)}) async-start(f32[8,512,64]{1,2,0:T(8,128)} %stack.15), calls=%async_computation | async-start | bytes 2097152 | tf_op jit(solution)/shard_map/all_to_all | solution.py:19
  20.2 34.1 %all-to-all-done = f32[8,512,64]{1,2,0:T(8,128)S(1)} async-done(((f32[8,512,64]{1,2,0:T(8,128)}), f32[8,512,64]{1,2,0:T(8,128)S(1)}, u32[]{:S(2)}, u32[]{:S(2)}) %all-to-all-start) | async-done | bytes 1048608 | tf_op jit(solution)/shard_map/all_to_all | solution.py:19
  55.4 3.7 all-to-all-start.1
  60.4 9.3 %all-gather.16.cloned.1.call-done = f32[1,512,512]{1,2,0:T(8,128)} async-done(((f32[1,512,64]{1,2,0:T(8,128)}), f32[1,512,512]{1,2,0:T(8,128)}) %all-gather.16.cloned.1.call-update) | async-done | bytes 1048592 | tf_op jit(solution)/shard_map/all_gather | solution.py:22
  69.7 2.3 fusion.29
  72.0 2.3 fusion.17
  74.3 2.8 fusion.19
  77.2 14.9 %all-to-all-done.1 = f32[8,512,64]{1,2,0:T(8,128)S(1)} async-done(((f32[8,512,64]{1,2,0:T(8,128)}), f32[8,512,64]{1,2,0:T(8,128)S(1)}, u32[]{:S(2)}, u32[]{:S(2)}) %all-to-all-start.1) | async-done | bytes 1048608 | tf_op jit(solution)/shard_map/all_to_all | solution.py:19
  92.2 7.5 %all-gather.22.cloned.1.call-done = f32[1,1,512,512]{2,3,1,0:T(8,128)} async-done(((f32[1,1,512,64]{2,3,1,0:T(8,128)}), f32[1,1,512,512]{2,3,1,0:T(8,128)}) %all-gather.22.cloned.1.call-update) | async-done | bytes 1048592 | tf_op jit(solution)/shard_map/all_gather | solution.py:21
  100.8 22.1 %all-gather.20.cloned.1.call-done = f32[1,512,512]{1,2,0:T(8,128)} async-done(((f32[1,512,64]{1,2,0:T(8,128)}), f32[1,512,512]{1,2,0:T(8,128)}) %all-gather.20.cloned.1.call-update) | async-done | bytes 1048592 | tf_op jit(solution)/shard_map/all_gather | solution.py:22
  122.8 2.3 fusion.26
  125.1 2.3 fusion.16
  127.4 20.4 %all-gather.14.cloned.1.call-done = f32[256,1024]{1,0:T(8,128)} async-done(((f32[256,128]{1,0:T(8,128)}), f32[256,1024]{1,0:T(8,128)}) %all-gather.14.cloned.1.call-update) | async-done | bytes 1048592 | tf_op jit(solution)/shard_map/all_gather | solution.py:44
  147.8 54.7 %all-reduce.5.cloned.1.call-done = f32[1024,256]{1,0:T(8,128)} async-done(((f32[1024,256]{1,0:T(8,128)}), f32[1024,256]{1,0:T(8,128)}) %all-reduce.5.cloned.1.call-update) | async-done | bytes 1048592 | tf_op jit(solution)/shard_map/psum | solution.py:36
  202.5 2.6 fusion.18
  205.2 2.8 fusion.22
  208.0 2.3 fusion.41
  211.5 49.1 %all-reduce.7.cloned.1.call-done = f32[1024,256]{1,0:T(8,128)} async-done(((f32[1024,256]{1,0:T(8,128)}), f32[1024,256]{1,0:T(8,128)}) %all-reduce.7.cloned.1.call-update) | async-done | bytes 1048592 | tf_op jit(solution)/shard_map/psum | solution.py:36
  262.4 47.6 %all-gather.26.cloned.1.call-done = f32[1,1024,1024]{2,1,0:T(8,128)} async-done(((f32[1,1024,128]{2,1,0:T(8,128)}), f32[1,1024,1024]{2,1,0:T(8,128)}) %all-gather.26.cloned.1.call-update) | async-done | bytes 4194320 | tf_op jit(solution)/shard_map/all_gather | solution.py:48
  310.0 10.3 %fusion.13 = f32[1024,256]{0,1:T(8,128)} fusion(f32[1024,256]{1,0:T(8,128)} %all-reduce.7.cloned.1.call-done, f32[1,1024,1024]{2,1,0:T(8,128)} %all-gather.26.cloned.1.call-done), kind=kOutput, calls=%fused_computation.7 | convolution fusion | flops 3221225472 | bytes 6291456 | tf_op jit(solution)/shard_map/dot_general | solution.py:10
  320.3 37.3 %all-gather.24.cloned.1.call-done = f32[1,1024,1024]{2,1,0:T(8,128)} async-done(((f32[1,1024,128]{2,1,0:T(8,128)}), f32[1,1024,1024]{2,1,0:T(8,128)}) %all-gather.24.cloned.1.call-update) | async-done | bytes 4194320 | tf_op jit(solution)/shard_map/all_gather | solution.py:45
  357.6 9.3 %fusion.10 = f32[1024,256]{0,1:T(8,128)S(1)} fusion(f32[1024,256]{0,1:T(8,128)} %fusion.13, f32[1024,256]{0,1:T(8,128)S(1)} %copy.8, f32[1024,256]{1,0:T(8,128)S(1)} %copy-done, f32[1,1024,1024]{2,1,0:T(8,128)} %all-gather.24.cloned.1.call-done), kind=kOutput, calls=%fused_computation.6 | convolution fusion | flops 3221749760 | bytes 8388608 | tf_op jit(solution)/shard_map/dot_general | solution.py:10
  (36 shorter events, 10.9 us)
Async XLA Ops:
  7.2 52.1 %all-gather.18.cloned.1.call-start = ((), (), s32[]{:S(2)}) async-start(), calls=%async_computation.6 | async-start | bytes 1179648 | tf_op jit(solution)/shard_map/all_gather | solution.py:21
  9.1 60.7 %all-gather.16.cloned.1.call-start = ((), (), s32[]{:S(2)}) async-start(), calls=%async_computation.5 | async-start | bytes 1179648 | tf_op jit(solution)/shard_map/all_gather | solution.py:22
  10.8 88.8 %all-gather.22.cloned.1.call-start = ((), (), s32[]{:S(2)}) async-start(), calls=%async_computation.8 | async-start | bytes 1179648 | tf_op jit(solution)/shard_map/all_gather | solution.py:21
  11.6 111.3 %all-gather.20.cloned.1.call-start = ((), (), s32[]{:S(2)}) async-start(), calls=%async_computation.7 | async-start | bytes 1179648 | tf_op jit(solution)/shard_map/all_gather | solution.py:22
  13.3 41.0 %all-to-all-start = ((f32[8,512,64]{1,2,0:T(8,128)}), f32[8,512,64]{1,2,0:T(8,128)S(1)}, u32[]{:S(2)}, u32[]{:S(2)}) async-start(f32[8,512,64]{1,2,0:T(8,128)} %stack.15), calls=%async_computation | async-start | bytes 2097152 | tf_op jit(solution)/shard_map/all_to_all | solution.py:19
  19.6 128.2 %all-gather.14.cloned.1.call-start = ((), (), s32[]{:S(2)}) async-start(), calls=%async_computation.3 | async-start | bytes 1179648 | tf_op jit(solution)/shard_map/all_gather | solution.py:44
  55.4 18.9 %copy-start.2 = (f32[2,256,256]{2,1,0:T(8,128)S(1)}, f32[2,256,256]{2,1,0:T(8,128)}, u32[]{:S(2)}) copy-start(f32[2,256,256]{2,1,0:T(8,128)} %param.6) | copy-start | bytes 1572868
  55.4 36.7 %all-to-all-start.1 = ((f32[8,512,64]{1,2,0:T(8,128)}), f32[8,512,64]{1,2,0:T(8,128)S(1)}, u32[]{:S(2)}, u32[]{:S(2)}) async-start(f32[8,512,64]{1,2,0:T(8,128)} %stack.17), calls=%async_computation.1 | async-start | bytes 2097152 | tf_op jit(solution)/shard_map/all_to_all | solution.py:19
  59.1 143.4 %all-reduce.5.cloned.1.call-start = ((), (), s32[]{:S(2)}) async-start(), calls=%async_computation.2 | async-start | bytes 2097152 | tf_op jit(solution)/shard_map/psum | solution.py:36
  77.1 183.4 %all-reduce.7.cloned.1.call-start = ((), (), s32[]{:S(2)}) async-start(), calls=%async_computation.4 | async-start | bytes 2097152 | tf_op jit(solution)/shard_map/psum | solution.py:36
  205.1 6.3 %copy-start = (f32[1024,256]{1,0:T(8,128)S(1)}, f32[1024,256]{1,0:T(8,128)}, u32[]{:S(2)}) copy-start(f32[1024,256]{1,0:T(8,128)} %all-reduce.5.cloned.1.call-done) | copy-start | bytes 3145732
  207.9 3.2 copy-start.1
  208.0 102.0 %all-gather.26.cloned.1.call-start = ((), (), s32[]{:S(2)}) async-start(), calls=%async_computation.10 | async-start | bytes 4718592 | tf_op jit(solution)/shard_map/all_gather | solution.py:48
  210.4 147.3 %all-gather.24.cloned.1.call-start = ((), (), s32[]{:S(2)}) async-start(), calls=%async_computation.9 | async-start | bytes 4718592 | tf_op jit(solution)/shard_map/all_gather | solution.py:45
Sparse Core Ops, SparseCore 0:
  9.6 31.3 all-gather.17
  42.5 27.1 all-gather.15
  71.9 27.6 all-gather.21
  101.1 21.6 all-gather.19
  124.3 23.4 all-gather.13
  151.3 51.1 all-reduce.4
  208.1 52.4 all-reduce.6
  262.1 47.8 all-gather.25
  311.6 45.9 all-gather.23
